TPU v7x, 32 devices: a whole 2x2x4 slice. The times are simulated.
32 devices in a mesh: grp: 4 (over z), wr: 8 (over y, x, core).
Axes of the slice: x: 2, y: 2, z: 4, core: 2. Of those that a mesh axis runs over, the one named last changes fastest.
Arguments:
- snapshots: float32 [256, 131072], P('wr', 'grp'), may hold values from -1300 to 1300
Outputs:
- basis: float32 [256, 131072], P(None, ('grp', 'wr'))
- r_scaled: float32 [256, 256], P(None, 'wr')
All inputs are finite; a program needn't handle non-finite values.
Results may differ from a plain program's by a relative error of at most 0.000073.
Values sent between devices are 32-bit elements; how exact they have to be, the bound alone decides.
No kernel may reach another device: no remote copies, remote signals or barrier semaphores. Data moves between devices by JAX's collectives and lax.ppermute only.
A program may use at most 64 MiB of HBM per device.

v0:
```python
import jax
import jax.numpy as jnp
from jax import lax
from jax.sharding import PartitionSpec as P


def partner(value, axis, stride):
    return lax.ppermute(value, axis, [(i, i ^ 1 << stride) for i in range(lax.axis_size(axis))])


def products(left, right):
    return lax.dot_general(
        left,
        right,
        (((1,), (1,)), ((), ())),
        precision=lax.Precision.HIGHEST,
        preferred_element_type=jnp.float32,
    )


def writer_levels(gram):
    for bit in range(lax.axis_size("wr").bit_length() - 1):
        gram = gram + partner(gram, "wr", bit)
    return gram


def group_levels(gram):
    for bit in range(lax.axis_size("grp").bit_length() - 1):
        gram = gram + partner(gram, "grp", bit)
    return gram


def body(snapshots):
    regrouped = lax.all_to_all(snapshots, "wr", split_axis=1, concat_axis=0, tiled=True)
    local_gram = products(regrouped, regrouped)
    total = writer_levels(group_levels(local_gram))
    lower = jnp.linalg.cholesky(total)
    cell_count = regrouped.shape[1] * lax.axis_size("grp") * lax.axis_size("wr")
    scale = jnp.sqrt(jnp.float32(cell_count))
    solved = lax.linalg.triangular_solve(lower, regrouped, left_side=True, lower=True)
    width = lower.shape[0] // lax.axis_size("wr")
    start = lax.axis_index("wr") * width
    columns = lax.dynamic_slice_in_dim(lower.T, start, width, 1)
    return (solved * scale, columns / scale)


def solution(mesh):
    placed = (P("wr", "grp"),)
    return jax.shard_map(
        body,
        mesh=mesh,
        in_specs=placed,
        out_specs=(P(None, ("grp", "wr")), P(None, "wr")),
        check_vma=False,
    )
```

profile of v0, /device:TPU:0, one launch (start us, length us, event | category | flops | bytes accessed | tf_op | source)
XLA Modules:
  0.0 169.7 jit_solution(11626017769321562424)
XLA Ops:
  0.6 2.5 %copy.22 = f32[4,8,8,4096]{3,2,0,1:T(8,128)S(1)} copy(f32[4,8,8,4096]{3,2,1,0:T(8,128)} %bitcast.50) | data formatting | bytes 8388608 | tf_op jit(solution)/shard_map/all_to_all | solution.py:34
  3.1 54.0 %all_to_all.19 = f32[32,8,4096]{2,0,1:T(8,128)S(1)} all-to-all(f32[32,8,4096]{2,0,1:T(8,128)S(1)} %bitcast.47), channel_id=1, replica_groups=mesh['grp'=4,'wr'=8] {'wr'}, dimensions={1} | all-to-all | bytes 8388608 | tf_op jit(solution)/shard_map/all_to_all | solution.py:34
  57.1 0.0 copy-start
  57.1 3.5 %fusion.10 = f32[256,256]{0,1:T(8,128)S(1)} fusion(f32[256,4096]{1,0:T(8,128)S(1)} %bitcast.45), kind=kOutput, calls=%fused_computation.32 | convolution fusion | flops 3221225472 | bytes 4456448 | tf_op jit(solution)/shard_map/dot_general | solution.py:12
  60.7 0.0 copy-done
  60.7 1.6 collective-permute-start
  62.3 5.9 %collective-permute-done = f32[256,256]{0,1:T(8,128)S(1)} collective-permute-done((f32[256,256]{0,1:T(8,128)S(1)}, f32[256,256]{0,1:T(8,128)S(1)}, u32[]{:S(2)}, u32[]{:S(2)}) %collective-permute-start) | collective-permute-done | bytes 262176 | tf_op jit(solution)/shard_map/ppermute | solution.py:8
  68.3 2.7 %collective-permute-start.1 = (f32[256,256]{0,1:T(8,128)S(1)}, f32[256,256]{0,1:T(8,128)S(1)}, u32[]{:S(2)}, u32[]{:S(2)}) collective-permute-start(f32[256,256]{0,1:T(8,128)S(1)} %add.40), channel_id=1, source_target_pairs={{0,16},{8,24},{16,0},{24,8},{1,17},{9,25},{17,1},{25,9},{2,18},{10... | collective-permute-start | bytes 786440 | tf_op jit(solution)/shard_map/ppermute | solution.py:8
  70.9 10.6 %collective-permute-done.1 = f32[256,256]{0,1:T(8,128)S(1)} collective-permute-done((f32[256,256]{0,1:T(8,128)S(1)}, f32[256,256]{0,1:T(8,128)S(1)}, u32[]{:S(2)}, u32[]{:S(2)}) %collective-permute-start.1) | collective-permute-done | bytes 262176 | tf_op jit(solution)/shard_map/ppermute | solution.py:8
  81.5 0.1 collective-permute-start.2
  81.6 1.5 collective-permute-done.2
  83.2 1.8 %collective-permute-start.3 = (f32[256,256]{0,1:T(8,128)S(1)}, f32[256,256]{0,1:T(8,128)S(1)}, u32[]{:S(2)}, u32[]{:S(2)}) collective-permute-start(f32[256,256]{0,1:T(8,128)S(1)} %add.42), channel_id=1, source_target_pairs={{0,2},{1,3},{2,0},{3,1},{4,6},{5,7},{6,4},{7,5},{8,10},{9,11},{10,... | collective-permute-start | bytes 786440 | tf_op jit(solution)/shard_map/ppermute | solution.py:8
  85.0 6.6 %collective-permute-done.3 = f32[256,256]{0,1:T(8,128)S(1)} collective-permute-done((f32[256,256]{0,1:T(8,128)S(1)}, f32[256,256]{0,1:T(8,128)S(1)}, u32[]{:S(2)}, u32[]{:S(2)}) %collective-permute-start.3) | collective-permute-done | bytes 262176 | tf_op jit(solution)/shard_map/ppermute | solution.py:8
  91.7 0.6 collective-permute-start.4
  92.2 4.0 %fusion.9 = (f32[4,32,4096]{2,1,0:T(8,128)}, f32[4,32,4096]{2,1,0:T(8,128)S(1)}) fusion(f32[8,32,4096]{2,1,0:T(8,128)} %bitcast.46), kind=kLoop, calls=%fused_computation.31 | loop fusion | bytes 8388608 | tf_op jit(solution)/shard_map/triangular_solve | solution.py:40
  96.3 3.0 %collective-permute-done.4 = f32[256,256]{0,1:T(8,128)S(1)} collective-permute-done((f32[256,256]{0,1:T(8,128)S(1)}, f32[256,256]{0,1:T(8,128)S(1)}, u32[]{:S(2)}, u32[]{:S(2)}) %collective-permute-start.4) | collective-permute-done | bytes 262176 | tf_op jit(solution)/shard_map/ppermute | solution.py:8
  99.3 0.1 copy.18
  99.5 11.7 %cholesky.50 = f32[128,128]{1,0:T(8,128)S(1)} custom-call(f32[128,128]{1,0:T(8,128)S(1)} %cholesky.118), custom_call_target="Cholesky" | custom-call | tf_op jit(solution)/shard_map/jit(cholesky)/cholesky | solution.py:37
  111.3 9.8 %custom-call.14 = f32[1,128,128]{1,2,0:T(8,128)S(1)} custom-call(f32[1,128,128]{2,1,0:T(8,128)S(1)} %get-tuple-element.27), custom_call_target="InvertDiagBlocksLowerTriangular" | custom-call | tf_op jit(solution)/shard_map/jit(cholesky)/cholesky | solution.py:37
  121.1 0.2 constant_dynamic-update-slice_fusion
  121.3 0.3 slice_subtract_fusion
  121.6 11.9 %cholesky.105 = f32[128,128]{1,0:T(8,128)S(1)} custom-call(f32[128,128]{1,0:T(8,128)S(1)} %slice_subtract_fusion), custom_call_target="Cholesky" | custom-call | tf_op jit(solution)/shard_map/jit(cholesky)/cholesky | solution.py:37
  133.5 0.6 compare_reduce_fusion
  135.4 0.1 triangular_solve.61
  135.4 3.8 %while.1 = (s32[]{:T(128)}, f32[256,256]{1,0:T(8,128)S(1)}, s32[2,2]{1,0:T(2,128)S(1)}, f32[2,128,128]{2,1,0:T(8,128)S(1)}, s32[]{:T(128)}) while((s32[]{:T(128)}, f32[256,256]{1,0:T(8,128)S(1)}, s32[2,2]{1,0:T(2,128)S(1)}, f32[2,128,128]{2,1,0:T(8,128)S(1)}, s32[]{:T(128)}) %tuple.29), condition=%wide.while_cond, body=%wide.while_body.sunk | while | flops 2 | bytes 131189 | solution.py:40
  135.4 0.6 fusion.19
  136.0 1.3 bitcast_dynamic-update-slice_fusion.2
  137.3 0.6 fusion.19
  137.9 1.3 bitcast_dynamic-update-slice_fusion.2
  139.2 19.7 %custom-call.15 = f32[2,128,128]{1,2,0:T(8,128)S(1)} custom-call(f32[2,128,128]{2,1,0:T(8,128)S(1)} %get-tuple-element.9), custom_call_target="InvertDiagBlocksLowerTriangular" | custom-call | tf_op jit(solution)/shard_map/triangular_solve | solution.py:40
  158.9 3.5 %fusion.4 = f32[128,4096]{1,0:T(8,128)S(1)} fusion(f32[128,4096]{1,0:T(8,128)} %bitcast.49, f32[2,128,128]{1,2,0:T(8,128)S(1)} %custom-call.15), kind=kOutput, calls=%fused_computation.14 | convolution fusion | flops 805306368 | bytes 4259840 | tf_op jit(solution)/shard_map/triangular_solve | solution.py:40
  162.4 2.0 %convolution_subtract_fusion = f32[128,4096]{1,0:T(8,128)S(1)} fusion(f32[128,4096]{1,0:T(8,128)S(1)} %bitcast.48, f32[128,4096]{1,0:T(8,128)S(1)} %fusion.4, f32[256,256]{1,0:T(8,128)S(1)} %get-tuple-element.76), kind=kOutput, calls=%fused_computation.2 | convolution fusion | flops 805830656 | bytes 6356992 | tf_op jit(solution)/shard_map/triangular_solve | solution.py:40
  164.4 1.9 %fusion.3 = f32[128,4096]{1,0:T(8,128)S(1)} fusion(f32[128,4096]{1,0:T(8,128)S(1)} %convolution_subtract_fusion, f32[2,128,128]{1,2,0:T(8,128)S(1)} %custom-call.15), kind=kOutput, calls=%fused_computation.12 | convolution fusion | flops 805306368 | bytes 4259840 | tf_op jit(solution)/shard_map/triangular_solve | solution.py:40
  166.3 2.7 %maximum_multiply_fusion = f32[256,4096]{1,0:T(8,128)} fusion(f32[128,4096]{1,0:T(8,128)S(1)} %fusion.3, f32[128,4096]{1,0:T(8,128)S(1)} %fusion.4), kind=kLoop, calls=%fused_computation.4 | loop fusion | flops 2097152 | bytes 8388608 | tf_op jit(solution)/shard_map/mul | solution.py:44
  169.1 0.6 multiply_bitcast_fusion
  (15 shorter events, 0.4 us)
Async XLA Ops:
  57.1 3.5 %copy-start = (f32[32,8,4096]{2,0,1:T(8,128)}, f32[32,8,4096]{2,0,1:T(8,128)S(1)}, u32[]{:S(2)}) copy-start(f32[32,8,4096]{2,0,1:T(8,128)S(1)} %all_to_all.19) | copy-start | bytes 12582916
  60.7 7.6 %collective-permute-start = (f32[256,256]{0,1:T(8,128)S(1)}, f32[256,256]{0,1:T(8,128)S(1)}, u32[]{:S(2)}, u32[]{:S(2)}) collective-permute-start(f32[256,256]{0,1:T(8,128)S(1)} %fusion.10), channel_id=1, source_target_pairs={{0,8},{8,0},{16,24},{24,16},{1,9},{9,1},{17,25},{25,17},{2,10},{10... | collective-permute-start | bytes 786440 | tf_op jit(solution)/shard_map/ppermute | solution.py:8
  68.3 13.2 %collective-permute-start.1 = (f32[256,256]{0,1:T(8,128)S(1)}, f32[256,256]{0,1:T(8,128)S(1)}, u32[]{:S(2)}, u32[]{:S(2)}) collective-permute-start(f32[256,256]{0,1:T(8,128)S(1)} %add.40), channel_id=1, source_target_pairs={{0,16},{8,24},{16,0},{24,8},{1,17},{9,25},{17,1},{25,9},{2,18},{10... | collective-permute-start | bytes 786440 | tf_op jit(solution)/shard_map/ppermute | solution.py:8
  81.5 1.6 collective-permute-start.2
  83.2 8.5 %collective-permute-start.3 = (f32[256,256]{0,1:T(8,128)S(1)}, f32[256,256]{0,1:T(8,128)S(1)}, u32[]{:S(2)}, u32[]{:S(2)}) collective-permute-start(f32[256,256]{0,1:T(8,128)S(1)} %add.42), channel_id=1, source_target_pairs={{0,2},{1,3},{2,0},{3,1},{4,6},{5,7},{6,4},{7,5},{8,10},{9,11},{10,... | collective-permute-start | bytes 786440 | tf_op jit(solution)/shard_map/ppermute | solution.py:8
  91.7 7.6 %collective-permute-start.4 = (f32[256,256]{0,1:T(8,128)S(1)}, f32[256,256]{0,1:T(8,128)S(1)}, u32[]{:S(2)}, u32[]{:S(2)}) collective-permute-start(f32[256,256]{0,1:T(8,128)S(1)} %add.43), channel_id=1, source_target_pairs={{0,4},{1,5},{2,6},{3,7},{4,0},{5,1},{6,2},{7,3},{8,12},{9,13},{10,... | collective-permute-start | bytes 786440 | tf_op jit(solution)/shard_map/ppermute | solution.py:8
where the time goes:
time: 170 us
  other arithmetic  57.4 us (34%)
  blocking collectives  54 us (32%)
  waiting for transfers between devices  27.6 us (16%)
  matrix products  11.4 us (7%)
  local copies, waits for them, and re-layouts  10.5 us (6%)
  starting transfers between devices  6.8 us (4%)
  between operations  1.98 us (1%)
    all_to_all x1, blocking collectives, body(): lax.all_to_all(snapshots, 'wr', split_axis=1, concat_axis=0, tiled=True)  54 us
    another operation x6, other arithmetic, body(): lower = jnp.linalg.cholesky(total)  34.1 us
    ppermute x5, waiting for transfers between devices, partner(): lax.ppermute(value, axis, [(i, i ^ 1 << stride) for i in range(lax.axis_s...  27.6 us
    another operation x3, other arithmetic, body(): lax.linalg.triangular_solve(lower, regrouped, left_side=True, lower=True)  19.7 us
    another operation x3, matrix products, body(): lax.linalg.triangular_solve(lower, regrouped, left_side=True, lower=True)  7.4 us
    ppermute x5, starting transfers between devices, partner(): lax.ppermute(value, axis, [(i, i ^ 1 << stride) for i in range(lax.axis_s...  6.8 us
    another operation x2, local copies, waits for them, and re-layouts, body(): lax.linalg.triangular_solve(lower, regrouped, left_side=True, lower=True)  4.08 us
    another operation x6, local copies, waits for them, and re-layouts  3.75 us
  transfers between devices with their start and end apart: 5, of which 5 were waited for; matrix products, arithmetic and copies ran while one was open for 2% of the time, Pallas kernels for 0%

commit v1 on v0

--- a/solution.py
+++ b/solution.py
@@ -31,7 +31,10 @@
 
 
 def body(snapshots):
-    regrouped = lax.all_to_all(snapshots, "wr", split_axis=1, concat_axis=0, tiled=True)
+    regrouped = jnp.concatenate(
+        lax.all_to_all(jnp.stack(jnp.split(snapshots, lax.axis_size("wr"), axis=1)), "wr", 0, 0),
+        axis=0,
+    )
     local_gram = products(regrouped, regrouped)
     total = writer_levels(group_levels(local_gram))
     lower = jnp.linalg.cholesky(total)

time: 170 us -> 177 us (1.041)
  local copies, waits for them, and re-layouts: 10.5 us -> 16.6 us
    unnamed x2 -> x9, local copies, waits for them, and re-layouts: 0.01 us -> 7.56 us
    all_to_all x1 -> x0, local copies, waits for them, and re-layouts: 2.47 us -> none  [body(): lax.all_to_all(snapshots, 'wr', split_axis=1, concat_axis=0, tiled=True)]
    another operation x6 -> x7, local copies, waits for them, and re-layouts: 3.75 us -> 4.83 us
where the time goes in v1:
time: 177 us; the launch traced here: 176 us
  other arithmetic  57.4 us (32%)
  blocking collectives  54 us (31%)
  waiting for transfers between devices  27.6 us (16%)
  local copies, waits for them, and re-layouts  16.6 us (9%)
  matrix products  11.4 us (6%)
  starting transfers between devices  6.8 us (4%)
  between operations  2.01 us (1%)
    all_to_all x1, blocking collectives, body(): lax.all_to_all(jnp.stack(jnp.split(snapshots, lax.axis_size('wr'), axis=1...  54 us
    another operation x6, other arithmetic, body(): lower = jnp.linalg.cholesky(total)  34.1 us
    ppermute x5, waiting for transfers between devices, partner(): lax.ppermute(value, axis, [(i, i ^ 1 << stride) for i in range(lax.axis_s...  27.6 us
    another operation x3, other arithmetic, body(): lax.linalg.triangular_solve(lower, regrouped, left_side=True, lower=True)  19.7 us
    unnamed x9, local copies, waits for them, and re-layouts  7.56 us
    another operation x3, matrix products, body(): lax.linalg.triangular_solve(lower, regrouped, left_side=True, lower=True)  7.4 us
    ppermute x5, starting transfers between devices, partner(): lax.ppermute(value, axis, [(i, i ^ 1 << stride) for i in range(lax.axis_s...  6.8 us
    another operation x2, local copies, waits for them, and re-layouts, body(): lax.linalg.triangular_solve(lower, regrouped, left_side=True, lower=True)  4.08 us
  transfers between devices with their start and end apart: 5, of which 5 were waited for; matrix products, arithmetic and copies ran while one was open for 2% of the time, Pallas kernels for 0%

profile of v1, /device:TPU:0, one launch (start us, length us, event | category | flops | bytes accessed | tf_op | source)
XLA Modules:
  0.0 175.9 jit_solution(10119740545232719052)
XLA Ops:
  0.6 1.1 bitcast_dynamic-update-slice_fusion.8
  1.7 1.1 bitcast_dynamic-update-slice_fusion.7
  2.8 1.1 bitcast_dynamic-update-slice_fusion.6
  3.9 1.1 bitcast_dynamic-update-slice_fusion.5
  5.0 1.1 bitcast_dynamic-update-slice_fusion.4
  6.1 1.1 bitcast_dynamic-update-slice_fusion.3
  7.1 1.1 bitcast_dynamic-update-slice_fusion.2
  8.2 1.1 bitcast_dynamic-update-slice_fusion.1
  9.3 54.0 %all_to_all.5 = f32[8,32,4096]{2,1,0:T(8,128)S(1)} all-to-all(f32[8,32,4096]{2,1,0:T(8,128)S(1)} %bitcast_dynamic-update-slice_fusion.1), channel_id=1, replica_groups=mesh['grp'=4,'wr'=8] {'wr'}, dimensions={0} | all-to-all | bytes 8388608 | tf_op jit(solution)/shard_map/all_to_all | solution.py:35
  63.3 0.0 copy-start
  63.3 3.5 %fusion.10 = f32[256,256]{0,1:T(8,128)S(1)} fusion(f32[256,4096]{1,0:T(8,128)S(1)} %bitcast.55), kind=kOutput, calls=%fused_computation.39 | convolution fusion | flops 3221225472 | bytes 4456448 | tf_op jit(solution)/shard_map/dot_general | solution.py:12
  66.9 0.0 copy-done
  66.9 1.6 collective-permute-start
  68.5 5.9 %collective-permute-done = f32[256,256]{0,1:T(8,128)S(1)} collective-permute-done((f32[256,256]{0,1:T(8,128)S(1)}, f32[256,256]{0,1:T(8,128)S(1)}, u32[]{:S(2)}, u32[]{:S(2)}) %collective-permute-start) | collective-permute-done | bytes 262176 | tf_op jit(solution)/shard_map/ppermute | solution.py:8
  74.5 2.7 %collective-permute-start.1 = (f32[256,256]{0,1:T(8,128)S(1)}, f32[256,256]{0,1:T(8,128)S(1)}, u32[]{:S(2)}, u32[]{:S(2)}) collective-permute-start(f32[256,256]{0,1:T(8,128)S(1)} %add.40), channel_id=1, source_target_pairs={{0,16},{8,24},{16,0},{24,8},{1,17},{9,25},{17,1},{25,9},{2,18},{10... | collective-permute-start | bytes 786440 | tf_op jit(solution)/shard_map/ppermute | solution.py:8
  77.1 10.6 %collective-permute-done.1 = f32[256,256]{0,1:T(8,128)S(1)} collective-permute-done((f32[256,256]{0,1:T(8,128)S(1)}, f32[256,256]{0,1:T(8,128)S(1)}, u32[]{:S(2)}, u32[]{:S(2)}) %collective-permute-start.1) | collective-permute-done | bytes 262176 | tf_op jit(solution)/shard_map/ppermute | solution.py:8
  87.7 0.1 collective-permute-start.2
  87.8 1.5 collective-permute-done.2
  89.4 1.8 %collective-permute-start.3 = (f32[256,256]{0,1:T(8,128)S(1)}, f32[256,256]{0,1:T(8,128)S(1)}, u32[]{:S(2)}, u32[]{:S(2)}) collective-permute-start(f32[256,256]{0,1:T(8,128)S(1)} %add.42), channel_id=1, source_target_pairs={{0,2},{1,3},{2,0},{3,1},{4,6},{5,7},{6,4},{7,5},{8,10},{9,11},{10,... | collective-permute-start | bytes 786440 | tf_op jit(solution)/shard_map/ppermute | solution.py:8
  91.2 6.6 %collective-permute-done.3 = f32[256,256]{0,1:T(8,128)S(1)} collective-permute-done((f32[256,256]{0,1:T(8,128)S(1)}, f32[256,256]{0,1:T(8,128)S(1)}, u32[]{:S(2)}, u32[]{:S(2)}) %collective-permute-start.3) | collective-permute-done | bytes 262176 | tf_op jit(solution)/shard_map/ppermute | solution.py:8
  97.9 0.6 collective-permute-start.4
  98.4 4.0 %fusion.9 = (f32[4,32,4096]{2,1,0:T(8,128)}, f32[4,32,4096]{2,1,0:T(8,128)S(1)}) fusion(f32[8,32,4096]{2,1,0:T(8,128)} %copy-done), kind=kLoop, calls=%fused_computation.38 | loop fusion | bytes 8388608 | tf_op jit(solution)/shard_map/triangular_solve | solution.py:43
  102.5 3.0 %collective-permute-done.4 = f32[256,256]{0,1:T(8,128)S(1)} collective-permute-done((f32[256,256]{0,1:T(8,128)S(1)}, f32[256,256]{0,1:T(8,128)S(1)}, u32[]{:S(2)}, u32[]{:S(2)}) %collective-permute-start.4) | collective-permute-done | bytes 262176 | tf_op jit(solution)/shard_map/ppermute | solution.py:8
  105.5 0.1 copy.5
  105.7 11.7 %cholesky.50 = f32[128,128]{1,0:T(8,128)S(1)} custom-call(f32[128,128]{1,0:T(8,128)S(1)} %cholesky.118), custom_call_target="Cholesky" | custom-call | tf_op jit(solution)/shard_map/jit(cholesky)/cholesky | solution.py:40
  117.5 9.8 %custom-call.14 = f32[1,128,128]{1,2,0:T(8,128)S(1)} custom-call(f32[1,128,128]{2,1,0:T(8,128)S(1)} %get-tuple-element.27), custom_call_target="InvertDiagBlocksLowerTriangular" | custom-call | tf_op jit(solution)/shard_map/jit(cholesky)/cholesky | solution.py:40
  127.3 0.2 constant_dynamic-update-slice_fusion
  127.5 0.3 slice_subtract_fusion
  127.8 11.9 %cholesky.105 = f32[128,128]{1,0:T(8,128)S(1)} custom-call(f32[128,128]{1,0:T(8,128)S(1)} %slice_subtract_fusion), custom_call_target="Cholesky" | custom-call | tf_op jit(solution)/shard_map/jit(cholesky)/cholesky | solution.py:40
  139.7 0.6 compare_reduce_fusion
  141.6 0.1 triangular_solve.61
  141.6 3.8 %while.1 = (s32[]{:T(128)}, f32[256,256]{1,0:T(8,128)S(1)}, s32[2,2]{1,0:T(2,128)S(1)}, f32[2,128,128]{2,1,0:T(8,128)S(1)}, s32[]{:T(128)}) while((s32[]{:T(128)}, f32[256,256]{1,0:T(8,128)S(1)}, s32[2,2]{1,0:T(2,128)S(1)}, f32[2,128,128]{2,1,0:T(8,128)S(1)}, s32[]{:T(128)}) %tuple.29), condition=%wide.while_cond, body=%wide.while_body.sunk | while | flops 2 | bytes 131189 | solution.py:43
  141.6 0.6 fusion.19
  142.2 1.3 bitcast_dynamic-update-slice_fusion.10
  143.5 0.6 fusion.19
  144.1 1.3 bitcast_dynamic-update-slice_fusion.10
  145.4 19.7 %custom-call.15 = f32[2,128,128]{1,2,0:T(8,128)S(1)} custom-call(f32[2,128,128]{2,1,0:T(8,128)S(1)} %get-tuple-element.9), custom_call_target="InvertDiagBlocksLowerTriangular" | custom-call | tf_op jit(solution)/shard_map/triangular_solve | solution.py:43
  165.1 3.5 %fusion.4 = f32[128,4096]{1,0:T(8,128)S(1)} fusion(f32[128,4096]{1,0:T(8,128)} %bitcast.57, f32[2,128,128]{1,2,0:T(8,128)S(1)} %custom-call.15), kind=kOutput, calls=%fused_computation.21 | convolution fusion | flops 805306368 | bytes 4259840 | tf_op jit(solution)/shard_map/triangular_solve | solution.py:43
  168.6 2.0 %convolution_subtract_fusion = f32[128,4096]{1,0:T(8,128)S(1)} fusion(f32[128,4096]{1,0:T(8,128)S(1)} %bitcast.56, f32[128,4096]{1,0:T(8,128)S(1)} %fusion.4, f32[256,256]{1,0:T(8,128)S(1)} %get-tuple-element.76), kind=kOutput, calls=%fused_computation.2 | convolution fusion | flops 805830656 | bytes 6356992 | tf_op jit(solution)/shard_map/triangular_solve | solution.py:43
  170.6 1.9 %fusion.3 = f32[128,4096]{1,0:T(8,128)S(1)} fusion(f32[128,4096]{1,0:T(8,128)S(1)} %convolution_subtract_fusion, f32[2,128,128]{1,2,0:T(8,128)S(1)} %custom-call.15), kind=kOutput, calls=%fused_computation.19 | convolution fusion | flops 805306368 | bytes 4259840 | tf_op jit(solution)/shard_map/triangular_solve | solution.py:43
  172.5 2.7 %maximum_multiply_fusion = f32[256,4096]{1,0:T(8,128)} fusion(f32[128,4096]{1,0:T(8,128)S(1)} %fusion.3, f32[128,4096]{1,0:T(8,128)S(1)} %fusion.4), kind=kLoop, calls=%fused_computation.3 | loop fusion | flops 2097152 | bytes 8388608 | tf_op jit(solution)/shard_map/mul | solution.py:47
  175.3 0.6 multiply_bitcast_fusion
  (15 shorter events, 0.4 us)
Async XLA Ops:
  63.3 3.5 %copy-start = (f32[8,32,4096]{2,1,0:T(8,128)}, f32[8,32,4096]{2,1,0:T(8,128)S(1)}, u32[]{:S(2)}) copy-start(f32[8,32,4096]{2,1,0:T(8,128)S(1)} %all_to_all.5) | copy-start | bytes 12582916
  66.9 7.6 %collective-permute-start = (f32[256,256]{0,1:T(8,128)S(1)}, f32[256,256]{0,1:T(8,128)S(1)}, u32[]{:S(2)}, u32[]{:S(2)}) collective-permute-start(f32[256,256]{0,1:T(8,128)S(1)} %fusion.10), channel_id=1, source_target_pairs={{0,8},{8,0},{16,24},{24,16},{1,9},{9,1},{17,25},{25,17},{2,10},{10... | collective-permute-start | bytes 786440 | tf_op jit(solution)/shard_map/ppermute | solution.py:8
  74.5 13.2 %collective-permute-start.1 = (f32[256,256]{0,1:T(8,128)S(1)}, f32[256,256]{0,1:T(8,128)S(1)}, u32[]{:S(2)}, u32[]{:S(2)}) collective-permute-start(f32[256,256]{0,1:T(8,128)S(1)} %add.40), channel_id=1, source_target_pairs={{0,16},{8,24},{16,0},{24,8},{1,17},{9,25},{17,1},{25,9},{2,18},{10... | collective-permute-start | bytes 786440 | tf_op jit(solution)/shard_map/ppermute | solution.py:8
  87.7 1.6 collective-permute-start.2
  89.4 8.5 %collective-permute-start.3 = (f32[256,256]{0,1:T(8,128)S(1)}, f32[256,256]{0,1:T(8,128)S(1)}, u32[]{:S(2)}, u32[]{:S(2)}) collective-permute-start(f32[256,256]{0,1:T(8,128)S(1)} %add.42), channel_id=1, source_target_pairs={{0,2},{1,3},{2,0},{3,1},{4,6},{5,7},{6,4},{7,5},{8,10},{9,11},{10,... | collective-permute-start | bytes 786440 | tf_op jit(solution)/shard_map/ppermute | solution.py:8
  97.9 7.6 %collective-permute-start.4 = (f32[256,256]{0,1:T(8,128)S(1)}, f32[256,256]{0,1:T(8,128)S(1)}, u32[]{:S(2)}, u32[]{:S(2)}) collective-permute-start(f32[256,256]{0,1:T(8,128)S(1)} %add.43), channel_id=1, source_target_pairs={{0,4},{1,5},{2,6},{3,7},{4,0},{5,1},{6,2},{7,3},{8,12},{9,13},{10,... | collective-permute-start | bytes 786440 | tf_op jit(solution)/shard_map/ppermute | solution.py:8
